TPU v7x, 32 devices: a whole 2x2x4 slice. The times are simulated.
32 devices in a mesh: grp: 2 (over x), row: 16 (over z, y, core).
Axes of the slice: x: 2, y: 2, z: 4, core: 2. Of those that a mesh axis runs over, the one named last changes fastest.
Arguments:
- coupling_features: bfloat16 [1024, 512, 128], P(('grp', 'row')), parts along dimension 0, may hold values from -6 to 6
- aligned_features: bfloat16 [256, 512, 256], P(('grp', 'row')), parts along dimension 0, may hold values from -6 to 6
- aligned_entry_flags: int32 [256, 512], P('grp'), parts along dimension 0, may hold values 0 or 1
- amino_real_flags: int32 [1024], P('grp'), parts along dimension 0, may hold values from 0 to 1, as said below
- coupling_offset_matrix: bfloat16 [128, 8], replicated, may hold values from -3.5 to 3.5
- lookup_matrices: bfloat16 [256, 1024], replicated, may hold values from -0.75 to 0.75
- aligned_final_matrix: bfloat16 [256, 256], replicated, may hold values from -0.375 to 0.375
- product_factor_matrices: bfloat16 [256, 64], replicated, may hold values from -0.375 to 0.375
- product_final_matrix: bfloat16 [1024, 128], replicated, may hold values from -1 to 1
- trio_factor_matrices: bfloat16 [128, 640], replicated, may hold values from -0.5 to 0.5
- trio_final_matrix: bfloat16 [128, 128], replicated, may hold values from -0.5 to 0.5
- feedforward_expand: bfloat16 [128, 512], replicated, may hold values from -0.5 to 0.5
- feedforward_shrink: bfloat16 [512, 128], replicated, may hold values from -0.25 to 0.25
Outputs:
- msa_out: bfloat16 [256, 512, 256], P(('grp', 'row')), parts along dimension 0
- coupling_refreshed: bfloat16 [1024, 512, 128], P(('grp', 'row')), parts along dimension 0
There are 2 independent parts, one for each index of `grp`. A program takes and returns all parts, laid end to end along the dimension named above; an argument that names none is the same for every part. Nothing has to cross between parts.
Inputs may be any that keep to these rules, and one draw needn't show every extreme that they name: `amino_real_flags`: 1 on a prefix of at least 256 residues and 0 on the rest, which is never empty.
All inputs are finite; a program needn't handle non-finite values.
Results may differ from a plain program's by a relative error of at most 0.008.
The roundings to bfloat16 on the way count: a program that leaves them out, or rounds other values in their place, can miss the bound.
Values may be sent and summed in bfloat16 or wider, within the bound.
No kernel may reach another device: no remote copies, remote signals or barrier semaphores. Data moves between devices by JAX's collectives and lax.ppermute only.
A program may use at most 192 MiB of HBM per device.

v0:
```python
import jax
import jax.numpy as jnp
from jax import lax
from jax.sharding import PartitionSpec as P

EPSILON = 1e-05


def standardize_features(values, dimension=-1):
    values = values.astype(jnp.float32)
    centered = values - jnp.mean(values, axis=dimension, keepdims=True)
    variance = jnp.mean(centered * centered, axis=dimension, keepdims=True)
    return centered * lax.rsqrt(variance + EPSILON)


def apply_matrix_map(values, weight):
    return jnp.einsum("...c,cd->...d", values, weight, preferred_element_type=jnp.float32)


def project_outer(raw_outer, product_final_matrix):
    row_total, col_total, left_width, right_width = raw_outer.shape
    flat = raw_outer.astype(jnp.bfloat16).reshape(row_total, col_total, left_width * right_width)
    return apply_matrix_map(flat, product_final_matrix)


def body(
    coupling_features,
    aligned_features,
    aligned_entry_flags,
    amino_real_flags,
    coupling_offset_matrix,
    lookup_matrices,
    aligned_final_matrix,
    product_factor_matrices,
    product_final_matrix,
    trio_factor_matrices,
    trio_final_matrix,
    feedforward_expand,
    feedforward_shrink,
):
    owned_aligned_lines = coupling_features.shape[0]
    residues = coupling_features.shape[1]
    pair_width = coupling_features.shape[2]
    owned_aligned_seqs = aligned_features.shape[0]
    aligned_feature_dim = aligned_features.shape[2]
    subspace_tally = coupling_offset_matrix.shape[1]
    subspace_dimension = aligned_feature_dim // subspace_tally
    outer_width = product_factor_matrices.shape[1] // 2
    placement_index = lax.axis_index("row")
    amino_real_valid = amino_real_flags.astype(jnp.float32)
    aligned_entry_valid = aligned_entry_flags.astype(jnp.float32) * amino_real_valid[None, :]
    my_residues = lax.dynamic_slice_in_dim(
        amino_real_valid, placement_index * owned_aligned_lines, owned_aligned_lines, 0
    )
    pair_valid = my_residues[:, None] * amino_real_valid[None, :]
    owned_aligned_flags = lax.dynamic_slice_in_dim(
        aligned_entry_valid, placement_index * owned_aligned_seqs, owned_aligned_seqs, 0
    )
    pair_normed = standardize_features(coupling_features).astype(jnp.bfloat16)
    bias_local = jnp.einsum(
        "ijc,ch->hij", pair_normed, coupling_offset_matrix, preferred_element_type=jnp.float32
    ).astype(jnp.bfloat16)
    tri_gates = jnp.einsum(
        "ijc,cd->dij",
        pair_normed,
        trio_factor_matrices[:, 0 : 4 * pair_width],
        preferred_element_type=jnp.float32,
    )
    left_tri = (
        jax.nn.sigmoid(tri_gates[0:pair_width])
        * tri_gates[pair_width : 2 * pair_width]
        * pair_valid[None]
    ).astype(jnp.bfloat16)
    right_tri = (
        jax.nn.sigmoid(tri_gates[2 * pair_width : 3 * pair_width])
        * tri_gates[3 * pair_width : 4 * pair_width]
        * pair_valid[None]
    ).astype(jnp.bfloat16)
    out_gate = jax.nn.sigmoid(
        apply_matrix_map(pair_normed, trio_factor_matrices[:, 4 * pair_width : 5 * pair_width])
    )
    left_full, right_full = (
        lax.all_to_all(left_tri, "row", split_axis=0, concat_axis=1, tiled=True),
        lax.all_to_all(right_tri, "row", split_axis=0, concat_axis=1, tiled=True),
    )
    tri_sum = jnp.einsum(
        "cik,cjk->cij", left_full, right_full, preferred_element_type=jnp.float32
    ).astype(jnp.bfloat16)
    tri_back = lax.all_to_all(tri_sum, "row", split_axis=1, concat_axis=0, tiled=True)
    tri_normed = standardize_features(tri_back, 0).astype(jnp.bfloat16)
    tri_update = out_gate * jnp.einsum(
        "cij,ce->ije", tri_normed, trio_final_matrix, preferred_element_type=jnp.float32
    )
    pair_one = coupling_features.astype(jnp.float32) + tri_update
    trans_hidden = jnp.maximum(
        apply_matrix_map(standardize_features(pair_one).astype(jnp.bfloat16), feedforward_expand),
        0.0,
    ).astype(jnp.bfloat16)
    pair_two = pair_one + apply_matrix_map(trans_hidden, feedforward_shrink)
    aligned_standardized = standardize_features(aligned_features).astype(jnp.bfloat16)
    lookup_factors_all = apply_matrix_map(aligned_standardized, lookup_matrices)
    asking_vectors = (
        (lookup_factors_all[..., 0:aligned_feature_dim] * subspace_dimension ** (-0.5))
        .astype(jnp.bfloat16)
        .reshape(owned_aligned_seqs, residues, subspace_tally, subspace_dimension)
    )
    lookup_subspaces = (
        lookup_factors_all[..., aligned_feature_dim : 2 * aligned_feature_dim]
        .astype(jnp.bfloat16)
        .reshape(owned_aligned_seqs, residues, subspace_tally, subspace_dimension)
    )
    content_subspaces = (
        lookup_factors_all[..., 2 * aligned_feature_dim : 3 * aligned_feature_dim]
        .astype(jnp.bfloat16)
        .reshape(owned_aligned_seqs, residues, subspace_tally, subspace_dimension)
    )
    aligned_sigmoid_factor = jax.nn.sigmoid(
        lookup_factors_all[..., 3 * aligned_feature_dim : 4 * aligned_feature_dim]
    )
    bias_piece = lax.all_gather(bias_local, "row", axis=1, tiled=True)
    asking_rows_sum = bias_piece.shape[1]
    affinity_matrix = jnp.einsum(
        "sihd,sjhd->shij", asking_vectors, lookup_subspaces, preferred_element_type=jnp.float32
    )
    affinity_matrix = affinity_matrix + bias_piece[None].astype(jnp.float32)
    affinity_matrix = jnp.where(
        owned_aligned_flags[:, None, None, :] > 0, affinity_matrix, -1000000000.0
    )
    attn_weights = jax.nn.softmax(affinity_matrix, axis=-1).astype(jnp.bfloat16)
    combined_features = jnp.einsum(
        "shij,sjhd->sihd", attn_weights, content_subspaces, preferred_element_type=jnp.float32
    )
    softmax_mixed_result = (
        combined_features.reshape(owned_aligned_seqs, asking_rows_sum, aligned_feature_dim)
        * aligned_sigmoid_factor
    ).astype(jnp.bfloat16)
    aligned_refreshed = aligned_features.astype(jnp.float32) + apply_matrix_map(
        softmax_mixed_result, aligned_final_matrix
    )
    product_standardized = standardize_features(aligned_refreshed).astype(jnp.bfloat16)
    product_factors = (
        jnp.einsum(
            "slm,mc->scl",
            product_standardized,
            product_factor_matrices,
            preferred_element_type=jnp.float32,
        )
        * owned_aligned_flags[:, None, :]
    )
    left_opm = product_factors[:, 0:outer_width].astype(jnp.bfloat16)
    right_opm = product_factors[:, outer_width : 2 * outer_width].astype(jnp.bfloat16)
    owned_crop_sites = lax.dynamic_slice_in_dim(
        aligned_entry_valid, placement_index * owned_aligned_lines, owned_aligned_lines, 1
    )
    coupling_tally = jnp.dot(
        owned_crop_sites.T, aligned_entry_valid, precision=lax.Precision.HIGHEST
    )
    left_res = lax.all_to_all(left_opm, "row", split_axis=2, concat_axis=0, tiled=True)
    right_all = lax.all_gather(right_opm, "row", axis=0, tiled=True)
    raw_total = jnp.einsum("sci,sdj->ijcd", left_res, right_all, preferred_element_type=jnp.float32)
    opm_sum = project_outer(raw_total, product_final_matrix)
    coupling_refreshed = (pair_two + opm_sum / jnp.maximum(coupling_tally, 1.0)[..., None]).astype(
        jnp.bfloat16
    )
    return (aligned_refreshed.astype(jnp.bfloat16), coupling_refreshed)


def solution(mesh):
    return jax.shard_map(
        body,
        mesh=mesh,
        in_specs=(
            P(("grp", "row"), None, None),
            P(("grp", "row"), None, None),
            P("grp", None),
            P("grp"),
            P(),
            P(),
            P(),
            P(),
            P(),
            P(),
            P(),
            P(),
            P(),
        ),
        out_specs=(P(("grp", "row"), None, None), P(("grp", "row"), None, None)),
        check_vma=False,
    )
```

profile of v0, /device:TPU:13, one launch (start us, length us, event | category | flops | bytes accessed | tf_op | source)
XLA Modules:
  0.0 526.1 jit_solution(14875835274564698252)
XLA Ops:
  7.2 0.0 all-gather.3.cloned.1.call-start
  7.2 6.5 %copy.75 = bf16[32,512,128]{1,2,0:T(8,128)(2,1)} copy(bf16[32,512,128]{2,1,0:T(8,128)(2,1)} %param.13) | data formatting | bytes 8388608 | tf_op args[0]
  13.7 3.1 convert_reduce_fusion
  16.8 0.3 copy-done.2
  17.1 1.3 fusion.12
  18.6 1.8 fusion.66
  20.4 0.0 all-gather.3.cloned.1.call-update
  20.4 0.1 dynamic_slice.10
  20.5 0.1 broadcast_multiply_fusion
  20.6 15.8 %convolution_bitcast_fusion = f32[512,32,512]{0,2,1:T(8,128)} fusion(bf16[32,512,128]{1,2,0:T(8,128)(2,1)} %copy.75, f32[32,512]{1,0:T(8,128)S(1)} %add_rsqrt_fusion.2, f32[32,512]{1,0:T(8,128)S(1)} %broadcast_multiply_fusion.3, bf16[128,640]{1,0:T(8,128)(2,1)S(1)} %copy-done.12), kind=kOutput, calls=%fused_computation.13 | convolution fusion | flops 2155872256 | bytes 38010880 | tf_op jit(solution)/shard_map/ijc,cd->dij/dot_general | solution.py:63
  36.4 15.5 %fusion.15 = (bf16[128,32,512]{0,2,1:T(8,128)(2,1)}, bf16[128,32,512]{0,2,1:T(8,128)(2,1)}) fusion(f32[512,32,512]{0,2,1:T(8,128)} %convolution_bitcast_fusion, f32[32,512]{1,0:T(8,128)S(1)} %broadcast_multiply_fusion), kind=kLoop, calls=%fused_computation.24 | loop fusion | flops 25165824 | bytes 42008576 | tf_op jit(solution)/shard_map/convert_element_type | solution.py:78
  51.9 8.0 %copy.84 = bf16[128,32,512]{2,1,0:T(8,128)(2,1)} copy(bf16[128,32,512]{0,2,1:T(8,128)(2,1)} %get-tuple-element.11) | data formatting | bytes 8388608 | tf_op jit(solution)/shard_map/convert_element_type | solution.py:73
  59.9 6.9 %all-to-all-start = ((bf16[128,32,512]{2,1,0:T(8,128)(2,1)}), bf16[128,32,512]{2,1,0:T(8,128)(2,1)}, u32[]{:S(2)}, u32[]{:S(2)}) async-start(bf16[128,32,512]{2,1,0:T(8,128)(2,1)} %copy.84), calls=%async_computation | async-start | bytes 8388608 | tf_op jit(solution)/shard_map/all_to_all | solution.py:83
  66.8 2.9 copy.70
  69.7 0.3 convert_reduce_fusion.1
  70.0 0.6 fusion.30
  70.6 8.2 %fusion.90 = (bf16[8,512,1024]{2,1,0:T(8,128)(2,1)S(1)}, f32[8,512,1024]{2,1,0:T(8,128)}) fusion(bf16[256,1024]{1,0:T(8,128)(2,1)S(1)} %copy-done, bf16[8,512,256]{1,2,0:T(8,128)(2,1)S(1)} %copy.70, f32[8,512]{1,0:T(8,128)S(1)} %add_rsqrt_fusion.4, f32[8,512]{1,0:T(8,128)S(1)} %broadcast_multiply_fusion.5), kind=kOutput, calls=%fused_computation.117 | convolution fusion | flops 2155872256 | bytes 27820032 | tf_op jit(solution)/shard_map/...c,cd->...d/dot_general | solution.py:17
  78.8 2.5 fusion.88
  81.3 3.9 copy.72
  85.2 4.0 fusion.39
  89.2 3.9 copy.73
  93.1 3.9 copy.74
  97.1 7.9 %copy.86 = bf16[128,32,512]{2,1,0:T(8,128)(2,1)} copy(bf16[128,32,512]{0,2,1:T(8,128)(2,1)} %get-tuple-element.10) | data formatting | bytes 8388608 | tf_op jit(solution)/shard_map/convert_element_type | solution.py:78
  105.1 0.0 all-gather.3.cloned.1.call-done
  105.1 8.7 %copy.77 = f32[8,512,512]{1,2,0:T(8,128)} copy(bf16[8,512,512]{2,0,1:T(8,128)(2,1)} %all-gather.3.cloned.1.call-done) | data formatting | bytes 12582912 | tf_op jit(solution)/shard_map/convert_element_type | solution.py:125
  113.8 39.5 %fusion.91 = (f32[8,8,512]{2,1,0:T(8,128)S(1)}, f32[8,8,512,512]{2,3,1,0:T(8,128)}) fusion(f32[8,512,512]{1,2,0:T(8,128)} %copy.77, pred[8,512]{1,0:T(8,128)(4,1)S(1)} %get-tuple-element.8, bf16[8,512,8,32]{1,3,2,0:T(8,128)(2,1)} %bitcast.101, bf16[8,512,8,32]{1,3,2,0:T(8,128)(2,1)} %bitcast.102), kind=kOutput, calls=%fused_computation.118 | convolution fusion | flops 1140851200 | bytes 79826944 | tf_op jit(solution)/shard_map/sub | solution.py:129
  153.3 6.6 %all-to-all-done = bf16[128,32,512]{2,1,0:T(8,128)(2,1)} async-done(((bf16[128,32,512]{2,1,0:T(8,128)(2,1)}), bf16[128,32,512]{2,1,0:T(8,128)(2,1)}, u32[]{:S(2)}, u32[]{:S(2)}) %all-to-all-start) | async-done | bytes 4194336 | tf_op jit(solution)/shard_map/all_to_all | solution.py:83
  159.9 5.4 %all-to-all-start.1 = ((bf16[128,32,512]{2,1,0:T(8,128)(2,1)}), bf16[128,32,512]{2,1,0:T(8,128)(2,1)}, u32[]{:S(2)}, u32[]{:S(2)}) async-start(bf16[128,32,512]{2,1,0:T(8,128)(2,1)} %copy.86), calls=%async_computation.1 | async-start | bytes 8388608 | tf_op jit(solution)/shard_map/all_to_all | solution.py:84
  165.3 24.5 %fusion.5 = f32[8,8,32,512]{3,2,1,0:T(8,128)} fusion(bf16[8,512,8,32]{1,3,2,0:T(8,128)(2,1)} %bitcast.110, f32[8,8,512,512]{2,3,1,0:T(8,128)} %get-tuple-element.21, f32[8,8,512]{2,1,0:T(8,128)S(1)} %get-tuple-element.20), kind=kOutput, calls=%fused_computation.10 | convolution fusion | flops 1107296256 | bytes 73531392 | tf_op jit(solution)/shard_map/shij,sjhd->sihd/dot_general | solution.py:130
  189.8 5.3 %copy.79 = f32[8,512,256]{2,1,0:T(8,128)} copy(f32[8,512,256]{1,2,0:T(8,128)} %bitcast.109) | data formatting | bytes 8388608 | tf_op jit(solution)/shard_map/reshape | solution.py:134
  195.2 4.9 copy.85
  200.1 5.8 %fusion.92 = (f32[8,512]{1,0:T(8,128)S(1)}, f32[8,512,256]{1,2,0:T(8,128)}) fusion(bf16[256,256]{1,0:T(8,128)(2,1)S(1)} %copy-done.17, f32[8,512,256]{2,1,0:T(8,128)S(1)} %copy-done.6, f32[8,512,1024]{2,1,0:T(8,128)} %get-tuple-element.19, bf16[8,512,256]{1,2,0:T(8,128)(2,1)S(1)} %copy.70), kind=kOutput, calls=%fused_computation.119 | convolution fusion | flops 545255424 | bytes 14827520 | tf_op jit(solution)/shard_map/...c,cd->...d/dot_general | solution.py:17
  205.9 51.8 %all-to-all-done.1 = bf16[128,32,512]{2,1,0:T(8,128)(2,1)} async-done(((bf16[128,32,512]{2,1,0:T(8,128)(2,1)}), bf16[128,32,512]{2,1,0:T(8,128)(2,1)}, u32[]{:S(2)}, u32[]{:S(2)}) %all-to-all-start.1) | async-done | bytes 4194336 | tf_op jit(solution)/shard_map/all_to_all | solution.py:84
  257.6 4.9 copy.87
  262.5 0.6 multiply_reduce_fusion.2
  263.1 0.1 copy-done.13
  263.3 0.6 fusion.62
  263.9 0.8 fusion.89
  264.6 1.7 copy.94
  266.3 3.1 reshape.139
  269.4 4.8 all-to-all-start.3
  274.1 5.8 %convolution_convert_fusion = bf16[8,512,512]{2,1,0:T(8,128)(2,1)S(1)} fusion(bf16[8,512,512]{2,1,0:T(8,128)(2,1)} %bitcast.107, bf16[8,512,512]{2,1,0:T(8,128)(2,1)} %bitcast.108), kind=kOutput, calls=%fused_computation.69 | convolution fusion | flops 2149580800 | bytes 12582912 | tf_op jit(solution)/shard_map/cik,cjk->cij/dot_general | solution.py:86
  280.0 4.4 copy.88
  284.3 6.0 %all-to-all-start.2 = ((bf16[8,512,512]{2,0,1:T(8,128)(2,1)}), bf16[8,512,512]{2,0,1:T(8,128)(2,1)}, u32[]{:S(2)}, u32[]{:S(2)}) async-start(bf16[8,512,512]{2,0,1:T(8,128)(2,1)} %copy.88), calls=%async_computation.2 | async-start | bytes 8388608 | tf_op jit(solution)/shard_map/all_to_all | solution.py:89
  290.3 0.4 all-gather.5.cloned.1.call-start
  290.8 0.3 all-gather.5.cloned.1.call-update
  291.1 0.4 convolution_maximum_fusion
  291.5 2.4 copy.101
  293.8 0.5 reshape.140
  294.3 0.8 copy.95
  295.1 1.1 copy.97
  296.2 111.9 %all-to-all-done.2 = bf16[8,512,512]{2,0,1:T(8,128)(2,1)} async-done(((bf16[8,512,512]{2,0,1:T(8,128)(2,1)}), bf16[8,512,512]{2,0,1:T(8,128)(2,1)}, u32[]{:S(2)}, u32[]{:S(2)}) %all-to-all-start.2) | async-done | bytes 4194336 | tf_op jit(solution)/shard_map/all_to_all | solution.py:89
  408.1 2.9 fusion.34
  411.0 3.4 multiply_reduce_fusion.1
  414.4 3.9 fusion.32
  418.4 4.7 fusion.93
  423.1 1.4 multiply_reduce_fusion
  424.6 1.8 copy-done.5
  426.4 0.0 all-gather.5.cloned.1.call-done
  426.4 20.5 %convert_bitcast_fusion = bf16[32,512,32,32]{1,0,2,3:T(8,128)(2,1)} fusion(bf16[128,32,512,1]{2,1,0,3:T(8,128)(2,1)} %bitcast.103, bf16[128,32,32]{0,2,1:T(8,128)(2,1)S(1)} %copy.97), kind=kOutput, calls=%fused_computation.5 | convolution fusion | flops 4311744512 | bytes 38010880 | tf_op jit(solution)/shard_map/sci,sdj->ijcd/dot_general | solution.py:160
  446.9 31.4 %copy.98 = bf16[32,512,32,32]{1,3,2,0:T(8,128)(2,1)} copy(bf16[32,512,32,32]{1,0,2,3:T(8,128)(2,1)} %convert_bitcast_fusion) | data formatting | bytes 67108864 | tf_op jit(solution)/shard_map/convert_element_type | solution.py:22
  478.3 14.3 %fusion.6 = f32[32,512,128]{1,2,0:T(8,128)} fusion(f32[32,512,128]{1,2,0:T(8,128)} %copy-done.5, f32[32,512]{1,0:T(8,128)S(1)} %add_rsqrt_fusion, f32[32,512]{1,0:T(8,128)S(1)} %broadcast_multiply_fusion.1, bf16[512,128]{1,0:T(8,128)(2,1)S(1)} %copy-done.18, bf16[128,512]{1,0:T(8,128)(2,1)S(1)} %copy-done.19), kind=kOutput, calls=%fused_computation.11 | convolution fusion | flops 4318035968 | bytes 17170432 | tf_op jit(solution)/shard_map/...c,cd->...d/dot_general | solution.py:17
  492.6 20.1 %add_convert_fusion = bf16[32,512,128]{1,2,0:T(8,128)(2,1)} fusion(f32[32,512,128]{1,2,0:T(8,128)} %copy-done.5, f32[32,512,128]{1,2,0:T(8,128)} %fusion.6, f32[32,512]{1,0:T(8,128)S(1)} %convolution_maximum_fusion, bf16[32,512,1024]{1,2,0:T(8,128)(2,1)} %bitcast.100, bf16[1024,128]{1,0:T(8,128)(2,1)S(1)} %copy-done.16), kind=kOutput, calls=%fused_computation.40 | convolution fusion | flops 4303355904 | bytes 54853632 | tf_op jit(solution)/shard_map/...c,cd->...d/dot_general | solution.py:17
  512.7 6.4 %copy.102 = bf16[32,512,128]{2,1,0:T(8,128)(2,1)} copy(bf16[32,512,128]{1,2,0:T(8,128)(2,1)} %add_convert_fusion) | data formatting | bytes 8388608
  (53 shorter events, 0.2 us)
Async XLA Ops:
  7.2 63.4 %copy-start = (bf16[256,1024]{1,0:T(8,128)(2,1)S(1)}, bf16[256,1024]{1,0:T(8,128)(2,1)}, u32[]{:S(2)}) copy-start(bf16[256,1024]{1,0:T(8,128)(2,1)} %param.18) | copy-start | bytes 1572868
  7.2 97.9 %all-gather.3.cloned.1.call-start = ((), (), s32[]{:S(2)}) async-start(), calls=%async_computation.4 | async-start | bytes 4456448 | tf_op jit(solution)/shard_map/all_gather | solution.py:120
  13.7 3.4 copy-start.2
  13.7 4.8 copy-start.20
  17.1 3.4 copy-start.7
  18.5 1.9 copy-start.15
  18.5 2.1 copy-start.12
  18.6 17.8 %copy-start.9 = (f32[32,512]{1,0:T(8,128)}, f32[32,512]{1,0:T(8,128)S(1)}, u32[]{:S(2)}) copy-start(f32[32,512]{1,0:T(8,128)S(1)} %add_rsqrt_fusion.2) | copy-start | bytes 196612
  59.9 100.1 %all-to-all-start = ((bf16[128,32,512]{2,1,0:T(8,128)(2,1)}), bf16[128,32,512]{2,1,0:T(8,128)(2,1)}, u32[]{:S(2)}, u32[]{:S(2)}) async-start(bf16[128,32,512]{2,1,0:T(8,128)(2,1)} %copy.84), calls=%async_computation | async-start | bytes 8388608 | tf_op jit(solution)/shard_map/all_to_all | solution.py:83
  97.1 7.9 %copy-start.11 = (s32[128,512]{1,0:T(8,128)S(1)}, s32[128,512]{1,0:T(8,128)}, u32[]{:S(2)}) copy-start(s32[128,512]{1,0:T(8,128)} %param.15) | copy-start | bytes 786436
  159.9 97.7 %all-to-all-start.1 = ((bf16[128,32,512]{2,1,0:T(8,128)(2,1)}), bf16[128,32,512]{2,1,0:T(8,128)(2,1)}, u32[]{:S(2)}, u32[]{:S(2)}) async-start(bf16[128,32,512]{2,1,0:T(8,128)(2,1)} %copy.86), calls=%async_computation.1 | async-start | bytes 8388608 | tf_op jit(solution)/shard_map/all_to_all | solution.py:84
  195.2 4.9 copy-start.6
  195.2 4.9 copy-start.17
  257.6 4.9 copy-start.4
  262.5 0.8 copy-start.13
  269.4 15.0 %all-to-all-start.3 = ((bf16[16,2,4096]{2,1,0:T(2,128)(2,1)}), bf16[16,2,4096]{2,1,0:T(2,128)(2,1)S(1)}, u32[]{:S(2)}, u32[]{:S(2)}) async-start(bf16[16,2,4096]{2,1,0:T(2,128)(2,1)} %reshape.139), calls=%async_computation.3 | async-start | bytes 524288 | tf_op jit(solution)/shard_map/all_to_all | solution.py:158
  284.3 123.8 %all-to-all-start.2 = ((bf16[8,512,512]{2,0,1:T(8,128)(2,1)}), bf16[8,512,512]{2,0,1:T(8,128)(2,1)}, u32[]{:S(2)}, u32[]{:S(2)}) async-start(bf16[8,512,512]{2,0,1:T(8,128)(2,1)} %copy.88), calls=%async_computation.2 | async-start | bytes 8388608 | tf_op jit(solution)/shard_map/all_to_all | solution.py:89
  290.3 136.0 %all-gather.5.cloned.1.call-start = ((), (), s32[]{:S(2)}) async-start(), calls=%async_computation.5 | async-start | bytes 4456448 | tf_op jit(solution)/shard_map/all_gather | solution.py:159
  408.1 6.3 %copy-start.14 = (bf16[128,128]{1,0:T(8,128)(2,1)S(1)}, bf16[128,128]{1,0:T(8,128)(2,1)}, u32[]{:S(2)}) copy-start(bf16[128,128]{1,0:T(8,128)(2,1)} %param.23) | copy-start | bytes 98308
  414.4 3.9 copy-start.3
  414.4 3.9 copy-start.8
  414.4 3.9 copy-start.10
  423.1 3.2 copy-start.5
  446.9 31.4 %copy-start.18 = (bf16[512,128]{1,0:T(8,128)(2,1)S(1)}, bf16[512,128]{1,0:T(8,128)(2,1)}, u32[]{:S(2)}) copy-start(bf16[512,128]{1,0:T(8,128)(2,1)} %param.25) | copy-start | bytes 393220
  446.9 31.4 %copy-start.19 = (bf16[128,512]{1,0:T(8,128)(2,1)S(1)}, bf16[128,512]{1,0:T(8,128)(2,1)}, u32[]{:S(2)}) copy-start(bf16[128,512]{1,0:T(8,128)(2,1)} %param.24) | copy-start | bytes 393220
  478.3 14.3 %copy-start.16 = (bf16[1024,128]{1,0:T(8,128)(2,1)S(1)}, bf16[1024,128]{1,0:T(8,128)(2,1)}, u32[]{:S(2)}) copy-start(bf16[1024,128]{1,0:T(8,128)(2,1)} %param.21) | copy-start | bytes 786436
  492.6 26.5 %copy-start.1 = (bf16[256,1024]{1,0:T(8,128)(2,1)S(1)}, bf16[256,1024]{1,0:T(8,128)(2,1)}, u32[]{:S(2)}) copy-start(bf16[256,1024]{1,0:T(8,128)(2,1)} %param.18) | copy-start | bytes 1572868
Sparse Core Ops, SparseCore 0:
  20.5 51.1 all-gather.2
  293.3 94.7 all-gather.4
where the time goes:
time: 534 us; the launch traced here: 526 us
  waiting for transfers between devices  171 us (32%)
  matrix products  166 us (31%)
  local copies, waits for them, and re-layouts  118 us (22%)
  other arithmetic  33.3 us (6%)
  starting transfers between devices  23.6 us (4%)
  between operations  14.6 us (3%)
    all_to_all x1, waiting for transfers between devices, body(): lax.all_to_all(tri_sum, 'row', split_axis=1, concat_axis=0, tiled=True)  112 us
    dot_general x5, matrix products, apply_matrix_map(): jnp.einsum('...c,cd->...d', values, weight, preferred_element_type=jnp.fl...  53.1 us
    all_to_all x1, waiting for transfers between devices, body(): lax.all_to_all(right_tri, 'row', split_axis=0, concat_axis=1, tiled=True)  51.8 us
    sub x1, matrix products, body(): attn_weights = jax.nn.softmax(affinity_matrix, axis=-1).astype(jnp.bfloat16)  39.5 us
    convert_element_type x1, local copies, waits for them, and re-layouts, project_outer(): raw_outer.astype(jnp.bfloat16)  31.4 us
    dot_general x1, matrix products, body(): jnp.einsum('shij,sjhd->sihd', attn_weights, content_subspaces, preferred_...  24.5 us
    unnamed x48, local copies, waits for them, and re-layouts  24 us
    dot_general x1, matrix products, body(): jnp.einsum('sci,sdj->ijcd', left_res, right_all, preferred_element_type=j...  20.5 us
  transfers between devices with their start and end apart: 6, of which 3 were waited for; matrix products, arithmetic and copies ran while one was open for 38% of the time, Pallas kernels for 0%

commit v1 on v0

--- a/solution.py
+++ b/solution.py
@@ -79,9 +79,13 @@
     out_gate = jax.nn.sigmoid(
         apply_matrix_map(pair_normed, trio_factor_matrices[:, 4 * pair_width : 5 * pair_width])
     )
+    rest_rings_by_axis = lambda message: jnp.concatenate(
+        lax.all_to_all(jnp.stack(jnp.split(message, lax.axis_size("row"), 0), axis=0), "row", 0, 0),
+        1,
+    )
     left_full, right_full = (
         lax.all_to_all(left_tri, "row", split_axis=0, concat_axis=1, tiled=True),
-        lax.all_to_all(right_tri, "row", split_axis=0, concat_axis=1, tiled=True),
+        rest_rings_by_axis(right_tri),
     )
     tri_sum = jnp.einsum(
         "cik,cjk->cij", left_full, right_full, preferred_element_type=jnp.float32

time: 534 us -> 526 us (0.985)
  waiting for transfers between devices: 171 us -> 159 us
    unnamed x48 -> x63, local copies, waits for them, and re-layouts: 24 us -> 41.6 us
    convert_element_type x1 -> x0, local copies, waits for them, and re-layouts: 7.92 us -> none  [body(): right_tri = (jax.nn.sigmoid(tri_gates[2 * pair_width:3 * pair_width]) * t...]
    all_to_all x1, waiting for transfers between devices: 6.6 us -> 0.01 us  [body(): lax.all_to_all(left_tri, 'row', split_axis=0, concat_axis=1, tiled=True)]
  transfers between devices with their start and end apart: 6 -> 6, of which waited for: 3 -> 2; matrix products, arithmetic and copies ran while one was open for 38% -> 41% of each run, Pallas kernels for 0% -> 0%
where the time goes in v1:
time: 526 us; the launch traced here: 516 us
  matrix products  164 us (31%)
  waiting for transfers between devices  159 us (30%)
  local copies, waits for them, and re-layouts  120 us (23%)
  other arithmetic  33.4 us (6%)
  starting transfers between devices  24.5 us (5%)
  between operations  14.7 us (3%)
    all_to_all x1, waiting for transfers between devices, body(): lax.all_to_all(tri_sum, 'row', split_axis=1, concat_axis=0, tiled=True)  112 us
    dot_general x5, matrix products, apply_matrix_map(): jnp.einsum('...c,cd->...d', values, weight, preferred_element_type=jnp.fl...  51.1 us
    all_to_all x1, waiting for transfers between devices, body(): lax.all_to_all(jnp.stack(jnp.split(message, lax.axis_size('row'), 0), axi...  46.9 us
    unnamed x63, local copies, waits for them, and re-layouts  41.6 us
    sub x1, matrix products, body(): attn_weights = jax.nn.softmax(affinity_matrix, axis=-1).astype(jnp.bfloat16)  39.5 us
    convert_element_type x1, local copies, waits for them, and re-layouts, project_outer(): raw_outer.astype(jnp.bfloat16)  31.4 us
    dot_general x1, matrix products, body(): jnp.einsum('shij,sjhd->sihd', attn_weights, content_subspaces, preferred_...  24.5 us
    dot_general x1, matrix products, body(): jnp.einsum('sci,sdj->ijcd', left_res, right_all, preferred_element_type=j...  20.5 us
  transfers between devices with their start and end apart: 6, of which 2 were waited for; matrix products, arithmetic and copies ran while one was open for 41% of the time, Pallas kernels for 0%

profile of v1, /device:TPU:13, one launch (start us, length us, event | category | flops | bytes accessed | tf_op | source)
XLA Modules:
  0.0 516.0 jit_solution(5639634824024660918)
XLA Ops:
  7.2 6.5 %copy.75 = bf16[32,512,128]{1,2,0:T(8,128)(2,1)} copy(bf16[32,512,128]{2,1,0:T(8,128)(2,1)} %param.13) | data formatting | bytes 8388608 | tf_op args[0]
  13.7 3.1 convert_reduce_fusion
  17.1 1.3 fusion.12
  18.6 1.8 fusion.71
  20.4 15.7 %convolution_bitcast_fusion = f32[512,32,512]{2,0,1:T(8,128)} fusion(bf16[32,512,128]{1,2,0:T(8,128)(2,1)} %copy.75, f32[32,512]{1,0:T(8,128)S(1)} %add_rsqrt_fusion.2, f32[32,512]{1,0:T(8,128)S(1)} %broadcast_multiply_fusion.3, bf16[128,640]{1,0:T(8,128)(2,1)S(1)} %copy-done.12), kind=kOutput, calls=%fused_computation.13 | convolution fusion | flops 2155872256 | bytes 38010880 | tf_op jit(solution)/shard_map/ijc,cd->dij/dot_general | solution.py:63
  36.2 15.6 %fusion.15 = (bf16[128,32,512]{2,0,1:T(8,128)(2,1)}, bf16[128,32,512]{2,0,1:T(8,128)(2,1)S(1)}) fusion(f32[512,32,512]{2,0,1:T(8,128)} %convolution_bitcast_fusion, f32[32,512]{1,0:T(8,128)S(1)} %broadcast_multiply_fusion), kind=kLoop, calls=%fused_computation.24 | loop fusion | flops 25165824 | bytes 42008576 | tf_op jit(solution)/shard_map/convert_element_type | solution.py:78
  51.8 4.4 copy.85
  56.2 6.9 %all-to-all-start = ((bf16[128,32,512]{2,1,0:T(8,128)(2,1)}), bf16[128,32,512]{2,1,0:T(8,128)(2,1)}, u32[]{:S(2)}, u32[]{:S(2)}) async-start(bf16[128,32,512]{2,1,0:T(8,128)(2,1)} %copy.85), calls=%async_computation | async-start | bytes 8388608 | tf_op jit(solution)/shard_map/all_to_all | solution.py:87
  63.0 2.9 copy.70
  66.2 0.6 fusion.30
  66.8 8.2 %fusion.111 = (bf16[8,512,1024]{2,1,0:T(8,128)(2,1)S(1)}, f32[8,512,1024]{2,1,0:T(8,128)}) fusion(bf16[256,1024]{1,0:T(8,128)(2,1)S(1)} %copy-done, bf16[8,512,256]{1,2,0:T(8,128)(2,1)S(1)} %copy.70, f32[8,512]{1,0:T(8,128)S(1)} %add_rsqrt_fusion.4, f32[8,512]{1,0:T(8,128)S(1)} %broadcast_multiply_fusion.5), kind=kOutput, calls=%fused_computation.151 | convolution fusion | flops 2155872256 | bytes 27820032 | tf_op jit(solution)/shard_map/...c,cd->...d/dot_general | solution.py:17
  75.0 2.5 fusion.109
  77.5 3.9 copy.72
  81.4 4.0 fusion.39
  85.4 4.0 copy.73
  89.4 3.9 copy.74
  93.4 1.8 fusion.90
  95.3 1.7 fusion.89
  96.9 1.7 fusion.88
  98.6 1.7 fusion.87
  100.3 1.7 fusion.86
  101.9 1.7 fusion.85
  103.6 1.7 fusion.84
  105.3 0.7 fusion.83
  106.0 0.7 fusion.82
  106.7 0.7 fusion.81
  107.4 0.7 fusion.80
  108.2 0.7 fusion.79
  108.9 0.7 fusion.78
  109.6 0.7 fusion.77
  110.3 0.7 fusion.76
  111.0 0.7 fusion.75
  111.8 8.7 %copy.77 = f32[8,512,512]{1,2,0:T(8,128)} copy(bf16[8,512,512]{2,0,1:T(8,128)(2,1)} %all-gather.3.cloned.1.call-done) | data formatting | bytes 12582912 | tf_op jit(solution)/shard_map/convert_element_type | solution.py:129
  120.5 39.5 %fusion.112 = (f32[8,8,512]{2,1,0:T(8,128)S(1)}, f32[8,8,512,512]{2,3,1,0:T(8,128)}) fusion(f32[8,512,512]{1,2,0:T(8,128)} %copy.77, pred[8,512]{1,0:T(8,128)(4,1)S(1)} %get-tuple-element.8, bf16[8,512,8,32]{1,3,2,0:T(8,128)(2,1)} %bitcast.164, bf16[8,512,8,32]{1,3,2,0:T(8,128)(2,1)} %bitcast.165), kind=kOutput, calls=%fused_computation.152 | convolution fusion | flops 1140851200 | bytes 79826944 | tf_op jit(solution)/shard_map/sub | solution.py:133
  160.0 6.4 %all-to-all-start.1 = ((bf16[16,8,32,512]{3,1,2,0:T(8,128)(2,1)}), bf16[16,8,32,512]{3,1,2,0:T(8,128)(2,1)}, u32[]{:S(2)}, u32[]{:S(2)}) async-start(bf16[16,8,32,512]{3,1,2,0:T(8,128)(2,1)} %fusion.75), calls=%async_computation.1 | async-start | bytes 8388608 | tf_op jit(solution)/shard_map/all_to_all | solution.py:83
  166.4 24.5 %fusion.5 = f32[8,8,32,512]{3,2,1,0:T(8,128)} fusion(bf16[8,512,8,32]{1,3,2,0:T(8,128)(2,1)} %bitcast.172, f32[8,8,512,512]{2,3,1,0:T(8,128)} %get-tuple-element.21, f32[8,8,512]{2,1,0:T(8,128)S(1)} %get-tuple-element.20), kind=kOutput, calls=%fused_computation.10 | convolution fusion | flops 1107296256 | bytes 73531392 | tf_op jit(solution)/shard_map/shij,sjhd->sihd/dot_general | solution.py:134
  190.9 5.3 %copy.79 = f32[8,512,256]{2,1,0:T(8,128)} copy(f32[8,512,256]{1,2,0:T(8,128)} %bitcast.171) | data formatting | bytes 8388608 | tf_op jit(solution)/shard_map/reshape | solution.py:138
  196.2 4.9 copy.86
  201.1 3.8 fusion.113
  204.9 0.6 multiply_reduce_fusion.2
  205.7 0.6 fusion.67
  206.3 0.8 fusion.110
  207.0 1.7 copy.94
  208.7 3.1 reshape.147
  211.7 46.9 %all-to-all-done.1 = bf16[16,8,32,512]{3,1,2,0:T(8,128)(2,1)} async-done(((bf16[16,8,32,512]{3,1,2,0:T(8,128)(2,1)}), bf16[16,8,32,512]{3,1,2,0:T(8,128)(2,1)}, u32[]{:S(2)}, u32[]{:S(2)}) %all-to-all-start.1) | async-done | bytes 4194336 | tf_op jit(solution)/shard_map/all_to_all | solution.py:83
  258.7 4.8 all-to-all-start.3
  263.5 6.4 %fusion.50 = bf16[8,512,512]{2,1,0:T(8,128)(2,1)S(1)} fusion(bf16[8,512,512]{2,1,0:T(8,128)(2,1)} %bitcast.170, bf16[8,512,512]{2,0,1:T(8,128)(2,1)} %bitcast.32), kind=kOutput, calls=%fused_computation.71 | convolution fusion | flops 2149580800 | bytes 12582912 | tf_op jit(solution)/shard_map/cik,cjk->cij/dot_general | solution.py:90
  269.9 4.4 copy.88
  274.2 6.0 %all-to-all-start.2 = ((bf16[8,512,512]{2,0,1:T(8,128)(2,1)}), bf16[8,512,512]{2,0,1:T(8,128)(2,1)}, u32[]{:S(2)}, u32[]{:S(2)}) async-start(bf16[8,512,512]{2,0,1:T(8,128)(2,1)} %copy.88), calls=%async_computation.2 | async-start | bytes 8388608 | tf_op jit(solution)/shard_map/all_to_all | solution.py:93
  281.4 2.4 copy.101
  284.2 0.8 copy.95
  285.0 1.1 copy.97
  286.1 111.9 %all-to-all-done.2 = bf16[8,512,512]{2,0,1:T(8,128)(2,1)} async-done(((bf16[8,512,512]{2,0,1:T(8,128)(2,1)}), bf16[8,512,512]{2,0,1:T(8,128)(2,1)}, u32[]{:S(2)}, u32[]{:S(2)}) %all-to-all-start.2) | async-done | bytes 4194336 | tf_op jit(solution)/shard_map/all_to_all | solution.py:93
  398.0 2.9 fusion.34
  400.9 3.4 multiply_reduce_fusion.1
  404.3 3.9 fusion.32
  408.3 4.7 fusion.114
  413.0 1.4 multiply_reduce_fusion
  414.5 1.8 copy-done.5
  416.3 20.5 %convert_bitcast_fusion = bf16[32,512,32,32]{1,0,2,3:T(8,128)(2,1)} fusion(bf16[128,32,512,1]{2,1,0,3:T(8,128)(2,1)} %bitcast.166, bf16[128,32,32]{0,2,1:T(8,128)(2,1)S(1)} %copy.97), kind=kOutput, calls=%fused_computation.5 | convolution fusion | flops 4311744512 | bytes 38010880 | tf_op jit(solution)/shard_map/sci,sdj->ijcd/dot_general | solution.py:164
  436.8 31.4 %copy.98 = bf16[32,512,32,32]{1,3,2,0:T(8,128)(2,1)} copy(bf16[32,512,32,32]{1,0,2,3:T(8,128)(2,1)} %convert_bitcast_fusion) | data formatting | bytes 67108864 | tf_op jit(solution)/shard_map/convert_element_type | solution.py:22
  468.2 14.3 %fusion.6 = f32[32,512,128]{1,2,0:T(8,128)} fusion(f32[32,512,128]{1,2,0:T(8,128)} %copy-done.5, f32[32,512]{1,0:T(8,128)S(1)} %add_rsqrt_fusion, f32[32,512]{1,0:T(8,128)S(1)} %broadcast_multiply_fusion.1, bf16[512,128]{1,0:T(8,128)(2,1)S(1)} %copy-done.18, bf16[128,512]{1,0:T(8,128)(2,1)S(1)} %copy-done.19), kind=kOutput, calls=%fused_computation.11 | convolution fusion | flops 4318035968 | bytes 17170432 | tf_op jit(solution)/shard_map/...c,cd->...d/dot_general | solution.py:17
  482.5 20.1 %add_convert_fusion = bf16[32,512,128]{1,2,0:T(8,128)(2,1)} fusion(f32[32,512,128]{1,2,0:T(8,128)} %copy-done.5, f32[32,512,128]{1,2,0:T(8,128)} %fusion.6, f32[32,512]{1,0:T(8,128)S(1)} %convolution_maximum_fusion, bf16[32,512,1024]{1,2,0:T(8,128)(2,1)} %bitcast.163, bf16[1024,128]{1,0:T(8,128)(2,1)S(1)} %copy-done.16), kind=kOutput, calls=%fused_computation.40 | convolution fusion | flops 4303355904 | bytes 54853632 | tf_op jit(solution)/shard_map/...c,cd->...d/dot_general | solution.py:17
  502.6 6.4 %copy.102 = bf16[32,512,128]{2,1,0:T(8,128)(2,1)} copy(bf16[32,512,128]{1,2,0:T(8,128)(2,1)} %add_convert_fusion) | data formatting | bytes 8388608
  (67 shorter events, 2.8 us)
Async XLA Ops:
  7.2 59.7 %copy-start = (bf16[256,1024]{1,0:T(8,128)(2,1)S(1)}, bf16[256,1024]{1,0:T(8,128)(2,1)}, u32[]{:S(2)}) copy-start(bf16[256,1024]{1,0:T(8,128)(2,1)} %param.18) | copy-start | bytes 1572868
  7.2 104.6 %all-gather.3.cloned.1.call-start = ((), (), s32[]{:S(2)}) async-start(), calls=%async_computation.4 | async-start | bytes 4456448 | tf_op jit(solution)/shard_map/all_gather | solution.py:124
  13.7 3.4 copy-start.2
  13.7 4.8 copy-start.20
  17.1 3.2 copy-start.7
  18.5 1.9 copy-start.15
  18.5 1.9 copy-start.12
  18.6 17.5 %copy-start.9 = (f32[32,512]{1,0:T(8,128)}, f32[32,512]{1,0:T(8,128)S(1)}, u32[]{:S(2)}) copy-start(f32[32,512]{1,0:T(8,128)S(1)} %add_rsqrt_fusion.2) | copy-start | bytes 196612
  56.2 103.8 %all-to-all-start = ((bf16[128,32,512]{2,1,0:T(8,128)(2,1)}), bf16[128,32,512]{2,1,0:T(8,128)(2,1)}, u32[]{:S(2)}, u32[]{:S(2)}) async-start(bf16[128,32,512]{2,1,0:T(8,128)(2,1)} %copy.85), calls=%async_computation | async-start | bytes 8388608 | tf_op jit(solution)/shard_map/all_to_all | solution.py:87
  85.4 7.9 %copy-start.11 = (s32[128,512]{1,0:T(8,128)S(1)}, s32[128,512]{1,0:T(8,128)}, u32[]{:S(2)}) copy-start(s32[128,512]{1,0:T(8,128)} %param.15) | copy-start | bytes 786436
  93.4 11.9 %copy-start.4 = (bf16[128,32,512]{2,0,1:T(8,128)(2,1)S(1)}, bf16[128,32,512]{2,0,1:T(8,128)(2,1)}, u32[]{:S(2)}) copy-start(bf16[128,32,512]{2,0,1:T(8,128)(2,1)} %get-tuple-element.10) | copy-start | bytes 12582916
  160.0 98.7 %all-to-all-start.1 = ((bf16[16,8,32,512]{3,1,2,0:T(8,128)(2,1)}), bf16[16,8,32,512]{3,1,2,0:T(8,128)(2,1)}, u32[]{:S(2)}, u32[]{:S(2)}) async-start(bf16[16,8,32,512]{3,1,2,0:T(8,128)(2,1)} %fusion.75), calls=%async_computation.1 | async-start | bytes 8388608 | tf_op jit(solution)/shard_map/all_to_all | solution.py:83
  196.2 4.9 copy-start.6
  196.2 4.9 copy-start.17
  204.9 0.8 copy-start.13
  258.7 15.5 %all-to-all-start.3 = ((bf16[16,2,4096]{2,1,0:T(2,128)(2,1)}), bf16[16,2,4096]{2,1,0:T(2,128)(2,1)S(1)}, u32[]{:S(2)}, u32[]{:S(2)}) async-start(bf16[16,2,4096]{2,1,0:T(2,128)(2,1)} %reshape.147), calls=%async_computation.3 | async-start | bytes 524288 | tf_op jit(solution)/shard_map/all_to_all | solution.py:162
  274.2 123.8 %all-to-all-start.2 = ((bf16[8,512,512]{2,0,1:T(8,128)(2,1)}), bf16[8,512,512]{2,0,1:T(8,128)(2,1)}, u32[]{:S(2)}, u32[]{:S(2)}) async-start(bf16[8,512,512]{2,0,1:T(8,128)(2,1)} %copy.88), calls=%async_computation.2 | async-start | bytes 8388608 | tf_op jit(solution)/shard_map/all_to_all | solution.py:93
  280.2 136.0 %all-gather.5.cloned.1.call-start = ((), (), s32[]{:S(2)}) async-start(), calls=%async_computation.5 | async-start | bytes 4456448 | tf_op jit(solution)/shard_map/all_gather | solution.py:163
  398.0 6.3 %copy-start.14 = (bf16[128,128]{1,0:T(8,128)(2,1)S(1)}, bf16[128,128]{1,0:T(8,128)(2,1)}, u32[]{:S(2)}) copy-start(bf16[128,128]{1,0:T(8,128)(2,1)} %param.23) | copy-start | bytes 98308
  404.3 3.9 copy-start.3
  404.3 3.9 copy-start.8
  404.3 3.9 copy-start.10
  413.0 3.2 copy-start.5
  436.8 31.4 %copy-start.18 = (bf16[512,128]{1,0:T(8,128)(2,1)S(1)}, bf16[512,128]{1,0:T(8,128)(2,1)}, u32[]{:S(2)}) copy-start(bf16[512,128]{1,0:T(8,128)(2,1)} %param.25) | copy-start | bytes 393220
  436.8 31.4 %copy-start.19 = (bf16[128,512]{1,0:T(8,128)(2,1)S(1)}, bf16[128,512]{1,0:T(8,128)(2,1)}, u32[]{:S(2)}) copy-start(bf16[128,512]{1,0:T(8,128)(2,1)} %param.24) | copy-start | bytes 393220
  468.2 14.4 %copy-start.16 = (bf16[1024,128]{1,0:T(8,128)(2,1)S(1)}, bf16[1024,128]{1,0:T(8,128)(2,1)}, u32[]{:S(2)}) copy-start(bf16[1024,128]{1,0:T(8,128)(2,1)} %param.21) | copy-start | bytes 786436
  482.5 26.5 %copy-start.1 = (bf16[256,1024]{1,0:T(8,128)(2,1)S(1)}, bf16[256,1024]{1,0:T(8,128)(2,1)}, u32[]{:S(2)}) copy-start(bf16[256,1024]{1,0:T(8,128)(2,1)} %param.18) | copy-start | bytes 1572868
Sparse Core Ops, SparseCore 0:
  20.5 54.6 all-gather.2
  283.2 94.7 all-gather.4
